TPU v7x, 32 devices: a whole 2x2x4 slice. The times are simulated.
32 devices in a mesh: guide: 2 (over core), tensor: 2 (over y), batch: 8 (over z, x).
Axes of the slice: x: 2, y: 2, z: 4, core: 2. Of those that a mesh axis runs over, the one named last changes fastest.
Arguments:
- latents: float32 [8, 16, 448], P('batch'), may hold values from -6 to 6
- lengths: int32 [8], P('batch'), may hold values from 1 to 448, 2240 in all
- timesteps: int32 [8], P('batch'), may hold values from 100 to 599
- guidance: float32 [8], P('batch'), may hold values from 1.5 to 6
- condition: float32 [2, 8, 1152], P('guide', 'batch'), may hold values from -6 to 6
- embed_weight: float32 [16, 1152], replicated, may hold values from -1.5 to 1.5
- modulation_weight: bfloat16 [2, 1152, 6, 1152], P(None, 'batch', None, 'tensor'), may hold values from -0.1875 to 0.1875
- final_modulation: bfloat16 [1152, 2, 1152], P('batch', None, 'tensor'), may hold values from -0.1875 to 0.1875
- qkv_weight: bfloat16 [2, 1152, 3, 1152], P(None, 'batch', None, 'tensor'), may hold values from -15 to 15
- proj_weight: bfloat16 [2, 1152, 1152], P(None, 'tensor', 'batch'), may hold values from -0.1875 to 0.1875
- up_weight: bfloat16 [2, 1152, 4608], P(None, 'batch', 'tensor'), may hold values from -0.1875 to 0.1875
- down_weight: bfloat16 [2, 4608, 1152], P(None, 'tensor', 'batch'), may hold values from -0.09375 to 0.09375
- output_weight: bfloat16 [1152, 16], replicated, may hold values from -0.1875 to 0.1875
Outputs:
- guided_noise: float32 [8, 16, 448], P('batch', 'guide', 'tensor')
- previous_latents: float32 [8, 16, 448], P('batch', 'guide', 'tensor')
Inputs may be any that keep to these rules, and one draw needn't show every extreme that they name: `lengths`: at least one request has exactly 448 live tokens; all requests together have 8 * 448 * 5 // 8.
All inputs are finite; a program needn't handle non-finite values. No bound on the sum of `lengths` on one device may be relied on, other than what follows from the above.
Results may differ from a plain program's by a relative error of at most 0.025.
Values may be sent and summed in bfloat16 or wider, within the bound.
No kernel may reach another device: no remote copies, remote signals or barrier semaphores. Data moves between devices by JAX's collectives and lax.ppermute only.
A program may use at most 128 MiB of HBM per device.

v0:
```python
import math
import jax
import jax.numpy as jnp
from jax import lax
from jax.sharding import PartitionSpec as P

HDIM = 72
TRAIN_STEPS = 1000
STRIDE = 20
norm_epsilon = 1e-06


def from_partner(block, axis, distance):
    count = lax.axis_size(axis)
    route = []
    for low in range(count):
        high = low | 1 << distance
        if high != low and high < count:
            route += [(low, high), (high, low)]
    return lax.ppermute(block, axis, route)


def layer_norm(values):
    center = values - jnp.mean(values, axis=-1, keepdims=True)
    spread = jnp.mean(center * center, axis=-1, keepdims=True)
    return center * lax.rsqrt(spread + norm_epsilon)


def modulate(values, shift, scale):
    return layer_norm(values) * (1.0 + scale[:, None, :]) + shift[:, None, :]


def position_table(row_count, width):
    rows_at = jnp.arange(row_count, dtype=jnp.int32).astype(jnp.float32)
    half_width = width // 2
    frequency = jnp.exp(
        jnp.arange(half_width, dtype=jnp.float32) * (-math.log(10000.0) / half_width)
    )
    angles = rows_at[:, None] * frequency[None, :]
    return jnp.concatenate([jnp.sin(angles), jnp.cos(angles)], axis=1)


def attend(operands):
    projected_item, key_live = operands
    score_scale = 1.0 / math.sqrt(HDIM)
    scores = (
        jnp.einsum(
            "qhd,khd->hqk",
            projected_item[:, 0],
            projected_item[:, 1],
            preferred_element_type=jnp.float32,
        )
        * score_scale
    )
    scores = jnp.where(key_live[None, None, :], scores, -jnp.inf)
    row_max = jnp.max(scores, axis=-1, keepdims=True)
    exp_scores = jnp.exp(scores - row_max)
    probabilities = (exp_scores / jnp.sum(exp_scores, axis=-1, keepdims=True)).astype(jnp.bfloat16)
    attended = jnp.einsum(
        "hqk,khd->qhd", probabilities, projected_item[:, 2], preferred_element_type=jnp.float32
    )
    return attended.astype(jnp.bfloat16).reshape(
        attended.shape[0], attended.shape[1] * attended.shape[2]
    )


def local(
    latents,
    lengths,
    timesteps,
    guidance,
    condition,
    embed_weight,
    modulation_weight,
    final_modulation,
    qkv_weight,
    proj_weight,
    up_weight,
    down_weight,
    output_weight,
):
    tensor_count = lax.axis_size("tensor")
    batch_count = lax.axis_size("batch")
    tensor_at = lax.axis_index("tensor")
    batch_at = lax.axis_index("batch")
    guide_at = lax.axis_index("guide")
    req_local, patch_size, max_len = latents.shape
    width = embed_weight.shape[1]
    layer_count = qkv_weight.shape[0]
    head_cols = qkv_weight.shape[3]
    heads_local = head_cols // HDIM
    rows_local = max_len // tensor_count
    width_piece = width // batch_count
    mod_count = 6 * layer_count + 2
    is_first = guide_at == 0

    def rows_product(activation, shard):
        return jnp.dot(
            activation,
            lax.all_gather(shard, "batch", axis=0, tiled=True),
            preferred_element_type=jnp.float32,
        )

    def cols_product(activation, shard):
        return jnp.dot(
            activation,
            lax.all_gather(shard, "batch", axis=1, tiled=True),
            preferred_element_type=jnp.float32,
        )

    cond_act = jax.nn.silu(condition[0]).astype(jnp.bfloat16)
    cond_all = lax.all_gather(cond_act, "batch", axis=0, tiled=True)
    cond_cols = lax.dynamic_slice_in_dim(cond_all, batch_at * width_piece, width_piece, 1)
    block_local = jnp.transpose(modulation_weight, (1, 0, 2, 3)).reshape(
        width_piece, 6 * layer_count * head_cols
    )
    mod_local = jnp.concatenate(
        [block_local, final_modulation.reshape(width_piece, 2 * head_cols)], axis=1
    )
    mod_mine = lax.psum_scatter(
        jnp.dot(cond_cols, mod_local, preferred_element_type=jnp.float32),
        "batch",
        scatter_dimension=0,
        tiled=True,
    )
    mod_full = lax.all_gather(
        mod_mine.reshape(req_local, mod_count, head_cols), "tensor", axis=2, tiled=True
    )
    positions = jnp.arange(max_len, dtype=jnp.int32)
    live_mask = positions[None, :] < lengths[:, None]
    own_start = tensor_at * rows_local
    own_latents = lax.dynamic_slice_in_dim(latents, own_start, rows_local, 2)
    own_live = lax.dynamic_slice_in_dim(live_mask, own_start, rows_local, 1)
    hidden_state = (
        jnp.einsum("rpl,pd->rld", latents, embed_weight, precision=lax.Precision.HIGHEST)
        + position_table(max_len, width)[None]
    )
    for layer_at in range(layer_count):
        modulation = mod_full[:, 6 * layer_at : 6 * layer_at + 6]
        normed = modulate(hidden_state, modulation[:, 0], modulation[:, 1]).astype(jnp.bfloat16)
        projected = rows_product(
            normed.reshape(req_local * max_len, width),
            qkv_weight[layer_at].reshape(width_piece, 3 * head_cols),
        ).astype(jnp.bfloat16)
        projected = projected.reshape(req_local, max_len, 3, heads_local, HDIM)
        attended = lax.map(attend, (projected, live_mask))
        branch = cols_product(
            attended.reshape(req_local * max_len, head_cols), proj_weight[layer_at]
        ).reshape(req_local, max_len, width)
        branch = lax.psum(branch.astype(jnp.bfloat16), "tensor").astype(jnp.float32)
        hidden_state = hidden_state + modulation[:, 2][:, None, :] * branch
        normed = modulate(hidden_state, modulation[:, 3], modulation[:, 4]).astype(jnp.bfloat16)
        hidden_units = jax.nn.gelu(
            rows_product(normed.reshape(req_local * max_len, width), up_weight[layer_at]),
            approximate=True,
        ).astype(jnp.bfloat16)
        branch = cols_product(hidden_units, down_weight[layer_at]).reshape(
            req_local, max_len, width
        )
        branch = lax.psum(branch.astype(jnp.bfloat16), "tensor").astype(jnp.float32)
        hidden_state = hidden_state + modulation[:, 5][:, None, :] * branch
    hidden_state = lax.dynamic_slice_in_dim(hidden_state, own_start, rows_local, 1)
    final_in = modulate(
        hidden_state, mod_full[:, 6 * layer_count], mod_full[:, 6 * layer_count + 1]
    ).astype(jnp.bfloat16)
    noise_own = jnp.einsum(
        "rld,dp->rpl", final_in, output_weight, preferred_element_type=jnp.float32
    )
    half_patch = patch_size // 2
    mine_noise = lax.dynamic_slice_in_dim(noise_own, guide_at * half_patch, half_patch, 1)
    other_noise = lax.dynamic_slice_in_dim(noise_own, (1 - guide_at) * half_patch, half_patch, 1)
    partner_noise = from_partner(other_noise, "guide", 0)
    cond_noise = jnp.where(is_first, mine_noise, partner_noise)
    uncond_noise = jnp.where(is_first, partner_noise, mine_noise)
    live_out = own_live[:, None, :]
    guided = uncond_noise + guidance[:, None, None] * (cond_noise - uncond_noise)
    guided = jnp.where(live_out, guided, 0.0)
    half_latents = lax.dynamic_slice_in_dim(own_latents, guide_at * half_patch, half_patch, 1)
    beta_values = jnp.linspace(0.0001, 0.02, TRAIN_STEPS, dtype=jnp.float32)
    alpha_bar = jnp.cumprod(1.0 - beta_values)
    step_ids = jnp.arange(TRAIN_STEPS, dtype=jnp.int32)
    alpha_now = jnp.sum(
        jnp.where(step_ids[None, :] == timesteps[:, None], alpha_bar[None, :], 0.0), axis=1
    )[:, None, None]
    alpha_prev = jnp.sum(
        jnp.where(step_ids[None, :] == (timesteps - STRIDE)[:, None], alpha_bar[None, :], 0.0),
        axis=1,
    )[:, None, None]
    start_est = (half_latents - jnp.sqrt(1.0 - alpha_now) * guided) / jnp.sqrt(alpha_now)
    previous = jnp.sqrt(alpha_prev) * start_est + jnp.sqrt(1.0 - alpha_prev) * guided
    previous = jnp.where(live_out, previous, 0.0)
    return (guided, previous)


def solution(mesh):
    in_specs = (
        P("batch", None, None),
        P("batch"),
        P("batch"),
        P("batch"),
        P("guide", "batch", None),
        P(),
        P(None, "batch", None, "tensor"),
        P("batch", None, "tensor"),
        P(None, "batch", None, "tensor"),
        P(None, "tensor", "batch"),
        P(None, "batch", "tensor"),
        P(None, "tensor", "batch"),
        P(),
    )
    out_specs = (P("batch", "guide", "tensor"), P("batch", "guide", "tensor"))
    return jax.shard_map(local, mesh=mesh, in_specs=in_specs, out_specs=out_specs, check_vma=False)
```

profile of v0, /device:TPU:1, one launch (start us, length us, event | category | flops | bytes accessed | tf_op | source)
XLA Modules:
  0.0 909.3 jit_solution(10363798787262294825)
XLA Ops:
  7.9 25.4 %all-gather.6 = bf16[8,1,1152]{2,1,0:T(2,128)(2,1)S(1)} all-gather(bf16[1,1,1152]{2,1,0:T(2,128)(2,1)S(1)} %fusion.119), channel_id=1, replica_groups=mesh['guide'=2,'tensor'=2,'batch'=8] {'batch'}, dimensions={0}, use_global_device_ids=true | all-gather | bytes 20736 | tf_op jit(solution)/shard_map/all_gather | solution.py:112
  35.6 3.2 reshape.338
  39.2 2.7 fusion.58
  44.6 4.1 multiply_sine_fusion
  52.5 64.8 %all-reduce.16.cloned.1.call-done = f32[8,8064]{1,0:T(8,128)} async-done(((f32[8,8064]{1,0:T(8,128)}), f32[8,8064]{1,0:T(8,128)}) %all-reduce.16.cloned.1.call-update) | async-done | bytes 258064
  119.2 6.8 all_gather.31
  126.0 62.0 %slice_reduce_fusion.2 = (f32[1152]{0:T(1024)S(1)}, f32[1152]{0:T(1024)S(1)}, f32[1152]{0:T(1024)S(1)}, f32[1152]{0:T(1024)S(1)}, f32[1152]{0:T(1024)S(1)}, /*in...) fusion(f32[1,14,1152]{1,0,2:T(1,128)S(1)} %all_gather.31), kind=kLoop, calls=%fused_computation.104 | loop fusion | flops 5760 | bytes 129024 | tf_op jit(solution)/shard_map/slice | solution.py:161
  188.0 4.9 all-gather.16.cloned.1.call-done
  192.9 5.8 convolution_convert_fusion.1
  198.7 3.0 copy.43
  201.7 5.9 fusion.146
  207.6 3.9 fusion.65
  211.5 26.3 %all-gather.20.cloned.1.call-done = bf16[1,576,1152]{1,2,0:T(8,128)(2,1)} async-done(((bf16[1,576,144]{1,2,0:T(8,128)(2,1)}), bf16[1,576,1152]{1,2,0:T(8,128)(2,1)}) %all-gather.20.cloned.1.call-update) | async-done | bytes 1327120 | tf_op jit(solution)/shard_map/all_gather | solution.py:107
  237.8 3.5 fusion.50
  244.3 35.8 %all-reduce.8.cloned.1.call-done = bf16[1,448,1152]{2,1,0:T(8,128)(2,1)} async-done(((bf16[1,448,1152]{2,1,0:T(8,128)(2,1)}), bf16[1,448,1152]{2,1,0:T(8,128)(2,1)}) %all-reduce.8.cloned.1.call-update) | async-done | bytes 1032208 | tf_op jit(solution)/shard_map/psum | solution.py:150
  280.1 2.2 fusion.140
  282.8 85.9 %all-gather.22.cloned.1.call-done = bf16[1,1152,2304]{2,1,0:T(8,128)(2,1)} async-done(((bf16[1,144,2304]{2,1,0:T(8,128)(2,1)}), bf16[1,1152,2304]{2,1,0:T(8,128)(2,1)}) %all-gather.22.cloned.1.call-update) | async-done | bytes 5308432 | tf_op jit(solution)/shard_map/all_gather | solution.py:100
  368.6 87.5 %all-gather.24.cloned.1.call-done = bf16[1,2304,1152]{1,2,0:T(8,128)(2,1)} async-done(((bf16[1,2304,144]{1,2,0:T(8,128)(2,1)}), bf16[1,2304,1152]{1,2,0:T(8,128)(2,1)}) %all-gather.24.cloned.1.call-update) | async-done | bytes 5308432 | tf_op jit(solution)/shard_map/all_gather | solution.py:107
  456.2 10.9 %fusion.55 = bf16[1,448,1152]{2,1,0:T(8,128)(2,1)} fusion(bf16[1,2304,1152]{1,2,0:T(8,128)(2,1)} %all-gather.24.cloned.1.call-done, bf16[1,1152,2304]{2,1,0:T(8,128)(2,1)} %all-gather.22.cloned.1.call-done, f32[1,448,1152]{2,1,0:T(8,128)S(1)} %get-tuple-element.47, f32[1152]{0:T(1024)S(1)} %get-tuple-element.34, f32[1152]{0:T(1024)S(1)} %get-tuple-element.35, ...), kind=kOutput, calls=%fused_computation.54 | convolution fusion | flops 4768727040 | bytes 13726208 | tf_op jit(solution)/shard_map/dot_general | solution.py:105
  469.7 36.3 %all-reduce.10.cloned.1.call-done = bf16[1,448,1152]{2,1,0:T(8,128)(2,1)} async-done(((bf16[1,448,1152]{2,1,0:T(8,128)(2,1)}), bf16[1,448,1152]{2,1,0:T(8,128)(2,1)}) %all-reduce.10.cloned.1.call-update) | async-done | bytes 1032208 | tf_op jit(solution)/shard_map/psum | solution.py:160
  508.2 71.6 %all-gather.18.cloned.1.call-done = bf16[1152,1728]{1,0:T(8,128)(2,1)} async-done(((bf16[144,1728]{1,0:T(8,128)(2,1)}), bf16[1152,1728]{1,0:T(8,128)(2,1)}) %all-gather.18.cloned.1.call-update) | async-done | bytes 3981328 | tf_op jit(solution)/shard_map/all_gather | solution.py:100
  579.8 6.0 convolution_convert_fusion
  585.8 3.7 copy.46
  589.5 7.2 fusion.147
  596.7 4.9 fusion.64
  601.6 23.1 %all-gather.26.cloned.1.call-done = bf16[1,576,1152]{1,2,0:T(8,128)(2,1)} async-done(((bf16[1,576,144]{1,2,0:T(8,128)(2,1)}), bf16[1,576,1152]{1,2,0:T(8,128)(2,1)}) %all-gather.26.cloned.1.call-update) | async-done | bytes 1327120 | tf_op jit(solution)/shard_map/all_gather | solution.py:107
  624.7 3.6 fusion.51
  629.9 37.2 %all-reduce.12.cloned.1.call-done = bf16[1,448,1152]{2,1,0:T(8,128)(2,1)} async-done(((bf16[1,448,1152]{2,1,0:T(8,128)(2,1)}), bf16[1,448,1152]{2,1,0:T(8,128)(2,1)}) %all-reduce.12.cloned.1.call-update) | async-done | bytes 1032208 | tf_op jit(solution)/shard_map/psum | solution.py:150
  670.6 85.2 %all-gather.28.cloned.1.call-done = bf16[1,1152,2304]{2,1,0:T(8,128)(2,1)} async-done(((bf16[1,144,2304]{2,1,0:T(8,128)(2,1)}), bf16[1,1152,2304]{2,1,0:T(8,128)(2,1)}) %all-gather.28.cloned.1.call-update) | async-done | bytes 5308432 | tf_op jit(solution)/shard_map/all_gather | solution.py:100
  755.8 87.5 %all-gather.30.cloned.1.call-done = bf16[1,2304,1152]{1,2,0:T(8,128)(2,1)} async-done(((bf16[1,2304,144]{1,2,0:T(8,128)(2,1)}), bf16[1,2304,1152]{1,2,0:T(8,128)(2,1)}) %all-gather.30.cloned.1.call-update) | async-done | bytes 5308432 | tf_op jit(solution)/shard_map/all_gather | solution.py:107
  843.4 11.6 %fusion.52 = bf16[1,448,1152]{2,1,0:T(8,128)(2,1)} fusion(bf16[1,2304,1152]{1,2,0:T(8,128)(2,1)} %all-gather.30.cloned.1.call-done, bf16[1,1152,2304]{2,1,0:T(8,128)(2,1)} %all-gather.28.cloned.1.call-done, f32[1,448,1152]{2,1,0:T(8,128)} %copy-done.3, f32[1152]{0:T(1024)S(1)} %get-tuple-element.25, f32[1152]{0:T(1024)S(1)} %get-tuple-element.26, ...), kind=kOutput, calls=%fused_computation.53 | convolution fusion | flops 4768727040 | bytes 13726208 | tf_op jit(solution)/shard_map/dot_general | solution.py:105
  856.4 37.5 %all-reduce.14.cloned.1.call-done = bf16[1,448,1152]{2,1,0:T(8,128)(2,1)} async-done(((bf16[1,448,1152]{2,1,0:T(8,128)(2,1)}), bf16[1,448,1152]{2,1,0:T(8,128)(2,1)}) %all-reduce.14.cloned.1.call-update) | async-done | bytes 1032208 | tf_op jit(solution)/shard_map/psum | solution.py:160
  (109 shorter events, 30.1 us)
Async XLA Ops:
  7.2 41.5 %copy-start = (f32[16,1152]{1,0:T(8,128)S(1)}, f32[16,1152]{1,0:T(8,128)}, u32[]{:S(2)}) copy-start(f32[16,1152]{1,0:T(8,128)} %param.18) | copy-start | bytes 221188
  7.2 110.1 %all-reduce.16.cloned.1.call-start = ((), (), s32[]{:S(2)}) async-start(), calls=%async_computation.12 | async-start | bytes 516096
  35.6 3.3 copy-start.10
  38.8 3.1 copy-start.8
  41.9 151.1 %all-gather.16.cloned.1.call-start = ((), (), s32[]{:S(2)}) async-start(), calls=%async_computation | async-start | bytes 4644864 | tf_op jit(solution)/shard_map/all_gather | solution.py:100
  42.0 1.7 copy-start.11
  43.7 5.0 copy-start.12
  43.7 194.1 %all-gather.20.cloned.1.call-start = ((), (), s32[]{:S(2)}) async-start(), calls=%async_computation.6 | async-start | bytes 1658880 | tf_op jit(solution)/shard_map/all_gather | solution.py:107
  44.5 235.6 %all-reduce.8.cloned.1.call-start = ((), (), s32[]{:S(2)}) async-start(), calls=%async_computation.1 | async-start | bytes 2064384 | tf_op jit(solution)/shard_map/psum | solution.py:150
  50.8 142.1 %copy-start.2 = (f32[448,1152]{1,0:T(8,128)}, f32[448,1152]{1,0:T(8,128)S(1)}, u32[]{:S(2)}) copy-start(f32[448,1152]{1,0:T(8,128)S(1)} %get-tuple-element.59) | copy-start | bytes 6193156
  50.8 1.1 copy-start.14
  237.8 3.6 copy-start.6
  241.3 1.8 copy-start.7
  241.3 127.3 %all-gather.22.cloned.1.call-start = ((), (), s32[]{:S(2)}) async-start(), calls=%async_computation.7 | async-start | bytes 5971968 | tf_op jit(solution)/shard_map/all_gather | solution.py:100
  242.6 213.6 %all-gather.24.cloned.1.call-start = ((), (), s32[]{:S(2)}) async-start(), calls=%async_computation.8 | async-start | bytes 5971968 | tf_op jit(solution)/shard_map/all_gather | solution.py:107
  244.3 261.7 %all-reduce.10.cloned.1.call-start = ((), (), s32[]{:S(2)}) async-start(), calls=%async_computation.2 | async-start | bytes 2064384 | tf_op jit(solution)/shard_map/psum | solution.py:160
  467.1 112.7 %all-gather.18.cloned.1.call-start = ((), (), s32[]{:S(2)}) async-start(), calls=%async_computation.3 | async-start | bytes 4644864 | tf_op jit(solution)/shard_map/all_gather | solution.py:100
  468.7 156.0 %all-gather.26.cloned.1.call-start = ((), (), s32[]{:S(2)}) async-start(), calls=%async_computation.9 | async-start | bytes 1658880 | tf_op jit(solution)/shard_map/all_gather | solution.py:107
  469.5 197.7 %all-reduce.12.cloned.1.call-start = ((), (), s32[]{:S(2)}) async-start(), calls=%async_computation.4 | async-start | bytes 2064384 | tf_op jit(solution)/shard_map/psum | solution.py:150
  506.0 1.7 copy-start.5
  628.3 127.5 %all-gather.28.cloned.1.call-start = ((), (), s32[]{:S(2)}) async-start(), calls=%async_computation.10 | async-start | bytes 5971968 | tf_op jit(solution)/shard_map/all_gather | solution.py:100
  629.1 214.3 %all-gather.30.cloned.1.call-start = ((), (), s32[]{:S(2)}) async-start(), calls=%async_computation.11 | async-start | bytes 5971968 | tf_op jit(solution)/shard_map/all_gather | solution.py:107
  629.6 264.3 %all-reduce.14.cloned.1.call-start = ((), (), s32[]{:S(2)}) async-start(), calls=%async_computation.5 | async-start | bytes 2064384 | tf_op jit(solution)/shard_map/psum | solution.py:160
  668.9 1.3 copy-start.3
  843.4 50.6 %copy-start.4 = (f32[1,448,1152]{2,1,0:T(8,128)S(1)}, f32[1,448,1152]{2,1,0:T(8,128)}, u32[]{:S(2)}) copy-start(f32[1,448,1152]{2,1,0:T(8,128)} %copy-done.3) | copy-start | bytes 6193156
  855.0 41.6 %copy-start.13 = (bf16[1152,16]{0,1:T(8,128)(2,1)S(1)}, bf16[1152,16]{0,1:T(8,128)(2,1)}, u32[]{:S(2)}) copy-start(bf16[1152,16]{0,1:T(8,128)(2,1)} %param.25) | copy-start | bytes 110596
  893.9 2.7 copy-start.9
  893.9 8.6 copy-start.1
  897.0 4.8 collective-permute-start
Sparse Core Ops, SparseCore 0:
  42.0 75.2 all-reduce.15
  119.7 73.1 all-gather.15
  195.3 42.4 all-gather.19
  241.5 38.6 all-reduce.7
  282.4 86.2 all-gather.21
  370.9 85.2 all-gather.23
  467.2 38.7 all-reduce.9
  508.4 71.3 all-gather.17
  582.2 42.4 all-gather.25
  628.4 38.6 all-reduce.11
  669.6 86.2 all-gather.27
  758.1 85.2 all-gather.29
  855.2 38.7 all-reduce.13
where the time goes:
time: 917 us; the launch traced here: 909 us
  waiting for transfers between devices  686 us (75%)
  other arithmetic  78.8 us (9%)
  matrix products  68.4 us (7%)
  blocking collectives  32.2 us (4%)
  local copies, waits for them, and re-layouts  23.4 us (3%)
  between operations  19.1 us (2%)
    all_gather x4, waiting for transfers between devices, rows_product(): lax.all_gather(shard, 'batch', axis=0, tiled=True)  248 us
    all_gather x4, waiting for transfers between devices, cols_product(): lax.all_gather(shard, 'batch', axis=1, tiled=True)  224 us
    psum x4, waiting for transfers between devices, local(): branch = lax.psum(branch.astype(jnp.bfloat16), 'tensor').astype(jnp.float32)  147 us
    unnamed x14, waiting for transfers between devices  66.8 us
    slice x1, other arithmetic, local(): hidden_state = hidden_state + modulation[:, 5][:, None, :] * branch  62 us
    dot_general x4, matrix products, cols_product(): jnp.dot(activation, lax.all_gather(shard, 'batch', axis=1, tiled=True), p...  29.7 us
    all_gather x1, blocking collectives, local(): cond_all = lax.all_gather(cond_act, 'batch', axis=0, tiled=True)  25.4 us
  transfers between devices with their start and end apart: 14, of which 13 were waited for; matrix products, arithmetic and copies ran while one was open for 14% of the time, Pallas kernels for 0%

commit v1 on v0

--- a/solution.py
+++ b/solution.py
@@ -8,6 +8,27 @@
 TRAIN_STEPS = 1000
 STRIDE = 20
 norm_epsilon = 1e-06
+
+
+def collect(x, axis, dim):
+    peers, index, extent = (lax.axis_size(axis), lax.axis_index(axis), x.shape[dim])
+    ahead = [(i, (i + 1) % peers) for i in range(peers)]
+    left = [(i, (i - 1) % peers) for i in range(peers)]
+    out = jnp.zeros((*x.shape[:dim], peers * extent, *x.shape[dim + 1 :]), x.dtype)
+    out = lax.dynamic_update_slice_in_dim(out, x, index * extent, axis=dim)
+    from_left = from_right = x
+    half = peers // 2
+    for step in range(1, half + 1):
+        from_left = lax.ppermute(from_left, axis, ahead)
+        out = lax.dynamic_update_slice_in_dim(
+            out, from_left, (index - step) % peers * extent, axis=dim
+        )
+        if step < peers - half:
+            from_right = lax.ppermute(from_right, axis, left)
+            out = lax.dynamic_update_slice_in_dim(
+                out, from_right, (index + step) % peers * extent, axis=dim
+            )
+    return out
 
 
 def from_partner(block, axis, distance):
@@ -102,11 +123,7 @@
         )
 
     def cols_product(activation, shard):
-        return jnp.dot(
-            activation,
-            lax.all_gather(shard, "batch", axis=1, tiled=True),
-            preferred_element_type=jnp.float32,
-        )
+        return jnp.dot(activation, collect(shard, "batch", 1), preferred_element_type=jnp.float32)
 
     cond_act = jax.nn.silu(condition[0]).astype(jnp.bfloat16)
     cond_all = lax.all_gather(cond_act, "batch", axis=0, tiled=True)

time: 917 us -> 776 us (0.85)
  waiting for transfers between devices: 686 us -> 431 us
  starting transfers between devices: 1.75 us -> 79.5 us
  local copies, waits for them, and re-layouts: 23.4 us -> 58.5 us
    all_gather x4 -> x0, waiting for transfers between devices: 224 us -> none  [cols_product(): lax.all_gather(shard, 'batch', axis=1, tiled=True)]
    ppermute x0 -> x28, waiting for transfers between devices: none -> 194 us  [the longest x16 149 us: collect(): from_left = lax.ppermute(from_left, axis, ahead)]
    all_gather x4, waiting for transfers between devices: 248 us -> 138 us  [rows_product(): lax.all_gather(shard, 'batch', axis=0, tiled=True)]
    psum x4, waiting for transfers between devices: 147 us -> 42.9 us  [local(): branch = lax.psum(branch.astype(jnp.bfloat16), 'tensor').astype(jnp.float32)]
    ppermute x0 -> x28, starting transfers between devices: none -> 78.4 us  [the longest x12 56.2 us: collect(): from_right = lax.ppermute(from_right, axis, left)]
    dynamic_update_slice x0 -> x32, local copies, waits for them, and re-layouts: none -> 27.3 us  [the longest x16 13.7 us: collect(): lax.dynamic_update_slice_in_dim(out, from_left, (index - step) % peers *...]
    unnamed x14 -> x10, waiting for transfers between devices: 66.8 us -> 55.9 us
  transfers between devices with their start and end apart: 14 -> 38, of which waited for: 13 -> 27; matrix products, arithmetic and copies ran while one was open for 14% -> 16% of each run, Pallas kernels for 0% -> 0%
where the time goes in v1:
time: 776 us; the launch traced here: 767 us
  waiting for transfers between devices  431 us (56%)
  starting transfers between devices  79.5 us (10%)
  other arithmetic  78.8 us (10%)
  matrix products  67.4 us (9%)
  local copies, waits for them, and re-layouts  58.5 us (8%)
  blocking collectives  32.2 us (4%)
  between operations  19.4 us (2%)
    ppermute x16, waiting for transfers between devices, collect(): from_left = lax.ppermute(from_left, axis, ahead)  149 us
    all_gather x4, waiting for transfers between devices, rows_product(): lax.all_gather(shard, 'batch', axis=0, tiled=True)  138 us
    slice x1, other arithmetic, local(): hidden_state = hidden_state + modulation[:, 5][:, None, :] * branch  62 us
    ppermute x12, starting transfers between devices, collect(): from_right = lax.ppermute(from_right, axis, left)  56.2 us
    unnamed x10, waiting for transfers between devices  55.9 us
    ppermute x12, waiting for transfers between devices, collect(): from_right = lax.ppermute(from_right, axis, left)  45.2 us
    psum x4, waiting for transfers between devices, local(): branch = lax.psum(branch.astype(jnp.bfloat16), 'tensor').astype(jnp.float32)  42.9 us
    dot_general x4, matrix products, cols_product(): jnp.dot(activation, collect(shard, 'batch', 1), preferred_element_type=jn...  29.6 us
  transfers between devices with their start and end apart: 38, of which 27 were waited for; matrix products, arithmetic and copies ran while one was open for 16% of the time, Pallas kernels for 0%

profile of v1, /device:TPU:1, one launch (start us, length us, event | category | flops | bytes accessed | tf_op | source)
XLA Modules:
  0.0 767.2 jit_solution(8205802288422102891)
XLA Ops:
  7.9 25.4 %all-gather.2 = bf16[8,1,1152]{2,1,0:T(2,128)(2,1)S(1)} all-gather(bf16[1,1,1152]{2,1,0:T(2,128)(2,1)S(1)} %fusion.107), channel_id=1, replica_groups=mesh['guide'=2,'tensor'=2,'batch'=8] {'batch'}, dimensions={0}, use_global_device_ids=true | all-gather | bytes 20736 | tf_op jit(solution)/shard_map/all_gather | solution.py:129
  64.3 55.1 %all-reduce.16.cloned.1.call-done = f32[8,8064]{1,0:T(8,128)} async-done(((f32[8,8064]{1,0:T(8,128)}), f32[8,8064]{1,0:T(8,128)}) %all-reduce.16.cloned.1.call-update) | async-done | bytes 258064
  121.3 6.8 all_gather.19
  128.1 62.0 %slice_reduce_fusion.2 = (f32[1152]{0:T(1024)S(1)}, f32[1152]{0:T(1024)S(1)}, f32[1152]{0:T(1024)S(1)}, f32[1152]{0:T(1024)S(1)}, f32[1152]{0:T(1024)S(1)}, /*in...) fusion(f32[1,14,1152]{1,0,2:T(1,128)S(1)} %all_gather.19), kind=kLoop, calls=%fused_computation.100 | loop fusion | flops 5760 | bytes 129024 | tf_op jit(solution)/shard_map/slice | solution.py:178
  200.3 5.6 collective-permute-done.6
  206.6 5.8 convolution_convert_fusion.1
  215.2 5.9 fusion.130
  231.3 4.2 collective-permute-start.8
  239.1 20.7 %collective-permute-done.7 = bf16[2304,144]{0,1:T(8,128)(2,1)S(1)} collective-permute-done((bf16[2304,144]{0,1:T(8,128)(2,1)S(1)}, bf16[2304,144]{0,1:T(8,128)(2,1)S(1)}, u32[]{:S(2)}, u32[]{:S(2)}) %collective-permute-start.7) | collective-permute-done | bytes 663584 | tf_op jit(solution)/shard_map/ppermute | solution.py:22
  262.1 14.2 %collective-permute-start.10 = (bf16[2304,144]{0,1:T(8,128)(2,1)S(1)}, bf16[2304,144]{0,1:T(8,128)(2,1)S(1)}, u32[]{:S(2)}, u32[]{:S(2)}) collective-permute-start(bf16[2304,144]{0,1:T(8,128)(2,1)S(1)} %collective-permute-done.8), channel_id=1, source_target_pairs={{0,7},{1,0},{2,1},{3,2},{4,3},{5,4},{6,5},{7,6},{8,15},{9,8},{10,9... | collective-permute-start | bytes 1990664 | tf_op jit(solution)/shard_map/ppermute | solution.py:27
  278.0 18.1 %collective-permute-done.9 = bf16[2304,144]{0,1:T(8,128)(2,1)S(1)} collective-permute-done((bf16[2304,144]{0,1:T(8,128)(2,1)S(1)}, bf16[2304,144]{0,1:T(8,128)(2,1)S(1)}, u32[]{:S(2)}, u32[]{:S(2)}) %collective-permute-start.9) | collective-permute-done | bytes 663584 | tf_op jit(solution)/shard_map/ppermute | solution.py:22
  299.1 14.4 %collective-permute-start.12 = (bf16[2304,144]{0,1:T(8,128)(2,1)S(1)}, bf16[2304,144]{0,1:T(8,128)(2,1)S(1)}, u32[]{:S(2)}, u32[]{:S(2)}) collective-permute-start(bf16[2304,144]{0,1:T(8,128)(2,1)S(1)} %collective-permute-done.10), channel_id=1, source_target_pairs={{0,7},{1,0},{2,1},{3,2},{4,3},{5,4},{6,5},{7,6},{8,15},{9,8},{10,9... | collective-permute-start | bytes 1990664 | tf_op jit(solution)/shard_map/ppermute | solution.py:27
  315.3 10.1 %collective-permute-done.11 = bf16[2304,144]{0,1:T(8,128)(2,1)S(1)} collective-permute-done((bf16[2304,144]{0,1:T(8,128)(2,1)S(1)}, bf16[2304,144]{0,1:T(8,128)(2,1)S(1)}, u32[]{:S(2)}, u32[]{:S(2)}) %collective-permute-start.11) | collective-permute-done | bytes 663584 | tf_op jit(solution)/shard_map/ppermute | solution.py:22
  330.7 13.5 %collective-permute-done.13 = bf16[2304,144]{0,1:T(8,128)(2,1)S(1)} collective-permute-done((bf16[2304,144]{0,1:T(8,128)(2,1)S(1)}, bf16[2304,144]{0,1:T(8,128)(2,1)S(1)}, u32[]{:S(2)}, u32[]{:S(2)}) %collective-permute-start.13) | collective-permute-done | bytes 663584 | tf_op jit(solution)/shard_map/ppermute | solution.py:22
  347.7 40.9 %all-gather.12.cloned.1.call-done = bf16[1,1152,2304]{2,1,0:T(8,128)(2,1)} async-done(((bf16[1,144,2304]{2,1,0:T(8,128)(2,1)}), bf16[1,1152,2304]{2,1,0:T(8,128)(2,1)}) %all-gather.12.cloned.1.call-update) | async-done | bytes 5308432 | tf_op jit(solution)/shard_map/all_gather | solution.py:121
  388.6 10.9 %fusion.42 = bf16[1,448,1152]{2,1,0:T(8,128)(2,1)} fusion(bf16[2304,1152]{0,1:T(8,128)(2,1)} %constant_dynamic-update-slice_fusion.16, bf16[1,1152,2304]{2,1,0:T(8,128)(2,1)} %all-gather.12.cloned.1.call-done, f32[1,448,1152]{2,1,0:T(8,128)S(1)} %get-tuple-element.47, f32[1152]{0:T(1024)S(1)} %get-tuple-element.34, f32[1152]{0:T(1024)S(1)} %get-tuple-element.35, ...), kind=kOutput, calls=%fused_computation.49 | convolution fusion | flops 4768727040 | bytes 13726208 | tf_op jit(solution)/shard_map/dot_general | solution.py:126
  401.2 4.5 collective-permute-start.14
  407.7 5.7 collective-permute-done.14
  430.0 4.4 collective-permute-done.19
  443.1 71.5 %all-gather.10.cloned.1.call-done = bf16[1152,1728]{1,0:T(8,128)(2,1)} async-done(((bf16[144,1728]{1,0:T(8,128)(2,1)}), bf16[1152,1728]{1,0:T(8,128)(2,1)}) %all-gather.10.cloned.1.call-update) | async-done | bytes 3981328 | tf_op jit(solution)/shard_map/all_gather | solution.py:121
  514.6 6.0 convolution_convert_fusion
  524.3 7.2 fusion.131
  547.7 19.4 %collective-permute-done.21 = bf16[2304,144]{0,1:T(8,128)(2,1)S(1)} collective-permute-done((bf16[2304,144]{0,1:T(8,128)(2,1)}, bf16[2304,144]{0,1:T(8,128)(2,1)S(1)}, u32[]{:S(2)}, u32[]{:S(2)}) %collective-permute-start.21) | collective-permute-done | bytes 663584 | tf_op jit(solution)/shard_map/ppermute | solution.py:22
  574.6 12.0 %collective-permute-done.23 = bf16[2304,144]{0,1:T(8,128)(2,1)S(1)} collective-permute-done((bf16[2304,144]{0,1:T(8,128)(2,1)S(1)}, bf16[2304,144]{0,1:T(8,128)(2,1)S(1)}, u32[]{:S(2)}, u32[]{:S(2)}) %collective-permute-start.23) | collective-permute-done | bytes 663584 | tf_op jit(solution)/shard_map/ppermute | solution.py:22
  586.7 18.4 %collective-permute-done.24 = bf16[2304,144]{0,1:T(8,128)(2,1)S(1)} collective-permute-done((bf16[2304,144]{0,1:T(8,128)(2,1)S(1)}, bf16[2304,144]{0,1:T(8,128)(2,1)S(1)}, u32[]{:S(2)}, u32[]{:S(2)}) %collective-permute-start.24) | collective-permute-done | bytes 663584 | tf_op jit(solution)/shard_map/ppermute | solution.py:27
  605.1 4.2 collective-permute-start.26
  611.1 21.5 %collective-permute-done.25 = bf16[2304,144]{0,1:T(8,128)(2,1)S(1)} collective-permute-done((bf16[2304,144]{0,1:T(8,128)(2,1)S(1)}, bf16[2304,144]{0,1:T(8,128)(2,1)S(1)}, u32[]{:S(2)}, u32[]{:S(2)}) %collective-permute-start.25) | collective-permute-done | bytes 663584 | tf_op jit(solution)/shard_map/ppermute | solution.py:22
  633.9 19.1 %collective-permute-done.26 = bf16[2304,144]{0,1:T(8,128)(2,1)S(1)} collective-permute-done((bf16[2304,144]{0,1:T(8,128)(2,1)S(1)}, bf16[2304,144]{0,1:T(8,128)(2,1)S(1)}, u32[]{:S(2)}, u32[]{:S(2)}) %collective-permute-start.26) | collective-permute-done | bytes 663584 | tf_op jit(solution)/shard_map/ppermute | solution.py:27
  653.8 15.2 %collective-permute-done.27 = bf16[2304,144]{0,1:T(8,128)(2,1)S(1)} collective-permute-done((bf16[2304,144]{0,1:T(8,128)(2,1)S(1)}, bf16[2304,144]{0,1:T(8,128)(2,1)S(1)}, u32[]{:S(2)}, u32[]{:S(2)}) %collective-permute-start.27) | collective-permute-done | bytes 663584 | tf_op jit(solution)/shard_map/ppermute | solution.py:22
  673.4 26.0 %all-gather.14.cloned.1.call-done = bf16[1,1152,2304]{2,1,0:T(8,128)(2,1)} async-done(((bf16[1,144,2304]{2,1,0:T(8,128)(2,1)}), bf16[1,1152,2304]{2,1,0:T(8,128)(2,1)}) %all-gather.14.cloned.1.call-update) | async-done | bytes 5308432 | tf_op jit(solution)/shard_map/all_gather | solution.py:121
  699.4 11.6 %fusion.43 = bf16[1,448,1152]{2,1,0:T(8,128)(2,1)} fusion(bf16[2304,1152]{0,1:T(8,128)(2,1)} %constant_dynamic-update-slice_fusion, bf16[1,1152,2304]{2,1,0:T(8,128)(2,1)} %all-gather.14.cloned.1.call-done, f32[1,448,1152]{2,1,0:T(8,128)} %copy-done.3, f32[1152]{0:T(1024)S(1)} %get-tuple-element.25, f32[1152]{0:T(1024)S(1)} %get-tuple-element.26, ...), kind=kOutput, calls=%fused_computation.50 | convolution fusion | flops 4768727040 | bytes 13726208 | tf_op jit(solution)/shard_map/dot_general | solution.py:126
  712.4 39.2 %all-reduce.14.cloned.1.call-done = bf16[1,448,1152]{2,1,0:T(8,128)(2,1)} async-done(((bf16[1,448,1152]{2,1,0:T(8,128)(2,1)}), bf16[1,448,1152]{2,1,0:T(8,128)(2,1)}) %all-reduce.14.cloned.1.call-update) | async-done | bytes 1032208 | tf_op jit(solution)/shard_map/psum | solution.py:177
  (193 shorter events, 148.4 us)
Async XLA Ops:
  7.2 112.2 %all-reduce.16.cloned.1.call-start = ((), (), s32[]{:S(2)}) async-start(), calls=%async_computation.8 | async-start | bytes 516096
  41.9 164.8 %all-gather.8.cloned.1.call-start = ((), (), s32[]{:S(2)}) async-start(), calls=%async_computation | async-start | bytes 4644864 | tf_op jit(solution)/shard_map/all_gather | solution.py:121
  43.7 301.4 %all-reduce.8.cloned.1.call-start = ((), (), s32[]{:S(2)}) async-start(), calls=%async_computation.1 | async-start | bytes 2064384 | tf_op jit(solution)/shard_map/psum | solution.py:167
  44.5 14.2 %collective-permute-start = (bf16[576,144]{0,1:T(8,128)(2,1)}, bf16[576,144]{0,1:T(8,128)(2,1)S(1)}, u32[]{:S(2)}, u32[]{:S(2)}) collective-permute-start(bf16[576,144]{0,1:T(8,128)(2,1)} %get-tuple-element.55), channel_id=1, source_target_pairs={{0,1},{1,2},{2,3},{3,4},{4,5},{5,6},{6,7},{7,0},{8,9},{9,10},{10,1... | collective-permute-start | bytes 497672 | tf_op jit(solution)/shard_map/ppermute | solution.py:22
  45.8 12.9 %collective-permute-start.1 = (bf16[576,144]{0,1:T(8,128)(2,1)}, bf16[576,144]{0,1:T(8,128)(2,1)S(1)}, u32[]{:S(2)}, u32[]{:S(2)}) collective-permute-start(bf16[576,144]{0,1:T(8,128)(2,1)} %get-tuple-element.55), channel_id=1, source_target_pairs={{0,7},{1,0},{2,1},{3,2},{4,3},{5,4},{6,5},{7,6},{8,15},{9,8},{10,9... | collective-permute-start | bytes 497672 | tf_op jit(solution)/shard_map/ppermute | solution.py:27
  58.7 131.4 %collective-permute-start.2 = (bf16[576,144]{0,1:T(8,128)(2,1)S(1)}, bf16[576,144]{0,1:T(8,128)(2,1)}, u32[]{:S(2)}, u32[]{:S(2)}) collective-permute-start(bf16[576,144]{0,1:T(8,128)(2,1)S(1)} %collective-permute-done), channel_id=1, source_target_pairs={{0,1},{1,2},{2,3},{3,4},{4,5},{5,6},{6,7},{7,0},{8,9},{9,10},{10,1... | collective-permute-start | bytes 497672 | tf_op jit(solution)/shard_map/ppermute | solution.py:22
  58.8 132.9 %collective-permute-start.3 = (bf16[576,144]{0,1:T(8,128)(2,1)S(1)}, bf16[576,144]{0,1:T(8,128)(2,1)}, u32[]{:S(2)}, u32[]{:S(2)}) collective-permute-start(bf16[576,144]{0,1:T(8,128)(2,1)S(1)} %collective-permute-done.1), channel_id=1, source_target_pairs={{0,7},{1,0},{2,1},{3,2},{4,3},{5,4},{6,5},{7,6},{8,15},{9,8},{10,9... | collective-permute-start | bytes 497672 | tf_op jit(solution)/shard_map/ppermute | solution.py:27
  190.1 8.6 %collective-permute-start.4 = (bf16[576,144]{0,1:T(8,128)(2,1)}, bf16[576,144]{0,1:T(8,128)(2,1)S(1)}, u32[]{:S(2)}, u32[]{:S(2)}) collective-permute-start(bf16[576,144]{0,1:T(8,128)(2,1)} %collective-permute-done.2), channel_id=1, source_target_pairs={{0,1},{1,2},{2,3},{3,4},{4,5},{5,6},{6,7},{7,0},{8,9},{9,10},{10,1... | collective-permute-start | bytes 497672 | tf_op jit(solution)/shard_map/ppermute | solution.py:22
  228.6 160.0 %all-gather.12.cloned.1.call-start = ((), (), s32[]{:S(2)}) async-start(), calls=%async_computation.6 | async-start | bytes 5971968 | tf_op jit(solution)/shard_map/all_gather | solution.py:121
  229.9 211.0 %all-reduce.10.cloned.1.call-start = ((), (), s32[]{:S(2)}) async-start(), calls=%async_computation.2 | async-start | bytes 2064384 | tf_op jit(solution)/shard_map/psum | solution.py:177
  231.3 28.5 %collective-permute-start.7 = (bf16[2304,144]{0,1:T(8,128)(2,1)S(1)}, bf16[2304,144]{0,1:T(8,128)(2,1)S(1)}, u32[]{:S(2)}, u32[]{:S(2)}) collective-permute-start(bf16[2304,144]{0,1:T(8,128)(2,1)S(1)} %get-tuple-element.50), channel_id=1, source_target_pairs={{0,1},{1,2},{2,3},{3,4},{4,5},{5,6},{6,7},{7,0},{8,9},{9,10},{10,1... | collective-permute-start | bytes 1990664 | tf_op jit(solution)/shard_map/ppermute | solution.py:22
  231.3 30.7 %collective-permute-start.8 = (bf16[2304,144]{0,1:T(8,128)(2,1)S(1)}, bf16[2304,144]{0,1:T(8,128)(2,1)S(1)}, u32[]{:S(2)}, u32[]{:S(2)}) collective-permute-start(bf16[2304,144]{0,1:T(8,128)(2,1)S(1)} %get-tuple-element.50), channel_id=1, source_target_pairs={{0,7},{1,0},{2,1},{3,2},{4,3},{5,4},{6,5},{7,6},{8,15},{9,8},{10,9... | collective-permute-start | bytes 1990664 | tf_op jit(solution)/shard_map/ppermute | solution.py:27
  259.9 36.3 %collective-permute-start.9 = (bf16[2304,144]{0,1:T(8,128)(2,1)S(1)}, bf16[2304,144]{0,1:T(8,128)(2,1)S(1)}, u32[]{:S(2)}, u32[]{:S(2)}) collective-permute-start(bf16[2304,144]{0,1:T(8,128)(2,1)S(1)} %collective-permute-done.7), channel_id=1, source_target_pairs={{0,1},{1,2},{2,3},{3,4},{4,5},{5,6},{6,7},{7,0},{8,9},{9,10},{10,1... | collective-permute-start | bytes 1990664 | tf_op jit(solution)/shard_map/ppermute | solution.py:22
  262.1 37.0 %collective-permute-start.10 = (bf16[2304,144]{0,1:T(8,128)(2,1)S(1)}, bf16[2304,144]{0,1:T(8,128)(2,1)S(1)}, u32[]{:S(2)}, u32[]{:S(2)}) collective-permute-start(bf16[2304,144]{0,1:T(8,128)(2,1)S(1)} %collective-permute-done.8), channel_id=1, source_target_pairs={{0,7},{1,0},{2,1},{3,2},{4,3},{5,4},{6,5},{7,6},{8,15},{9,8},{10,9... | collective-permute-start | bytes 1990664 | tf_op jit(solution)/shard_map/ppermute | solution.py:27
  296.1 29.2 %collective-permute-start.11 = (bf16[2304,144]{0,1:T(8,128)(2,1)S(1)}, bf16[2304,144]{0,1:T(8,128)(2,1)S(1)}, u32[]{:S(2)}, u32[]{:S(2)}) collective-permute-start(bf16[2304,144]{0,1:T(8,128)(2,1)S(1)} %collective-permute-done.9), channel_id=1, source_target_pairs={{0,1},{1,2},{2,3},{3,4},{4,5},{5,6},{6,7},{7,0},{8,9},{9,10},{10,1... | collective-permute-start | bytes 1990664 | tf_op jit(solution)/shard_map/ppermute | solution.py:22
  299.1 30.7 %collective-permute-start.12 = (bf16[2304,144]{0,1:T(8,128)(2,1)S(1)}, bf16[2304,144]{0,1:T(8,128)(2,1)S(1)}, u32[]{:S(2)}, u32[]{:S(2)}) collective-permute-start(bf16[2304,144]{0,1:T(8,128)(2,1)S(1)} %collective-permute-done.10), channel_id=1, source_target_pairs={{0,7},{1,0},{2,1},{3,2},{4,3},{5,4},{6,5},{7,6},{8,15},{9,8},{10,9... | collective-permute-start | bytes 1990664 | tf_op jit(solution)/shard_map/ppermute | solution.py:27
  325.4 18.7 %collective-permute-start.13 = (bf16[2304,144]{0,1:T(8,128)(2,1)S(1)}, bf16[2304,144]{0,1:T(8,128)(2,1)S(1)}, u32[]{:S(2)}, u32[]{:S(2)}) collective-permute-start(bf16[2304,144]{0,1:T(8,128)(2,1)S(1)} %collective-permute-done.11), channel_id=1, source_target_pairs={{0,1},{1,2},{2,3},{3,4},{4,5},{5,6},{6,7},{7,0},{8,9},{9,10},{10,1... | collective-permute-start | bytes 1990664 | tf_op jit(solution)/shard_map/ppermute | solution.py:22
  399.5 115.1 %all-gather.10.cloned.1.call-start = ((), (), s32[]{:S(2)}) async-start(), calls=%async_computation.3 | async-start | bytes 4644864 | tf_op jit(solution)/shard_map/all_gather | solution.py:121
  401.2 268.8 %all-reduce.12.cloned.1.call-start = ((), (), s32[]{:S(2)}) async-start(), calls=%async_computation.4 | async-start | bytes 2064384 | tf_op jit(solution)/shard_map/psum | solution.py:167
  401.2 12.2 %collective-permute-start.14 = (bf16[576,144]{0,1:T(8,128)(2,1)}, bf16[576,144]{0,1:T(8,128)(2,1)S(1)}, u32[]{:S(2)}, u32[]{:S(2)}) collective-permute-start(bf16[576,144]{0,1:T(8,128)(2,1)} %get-tuple-element.54), channel_id=1, source_target_pairs={{0,1},{1,2},{2,3},{3,4},{4,5},{5,6},{6,7},{7,0},{8,9},{9,10},{10,1... | collective-permute-start | bytes 497672 | tf_op jit(solution)/shard_map/ppermute | solution.py:22
  405.8 10.5 %collective-permute-start.15 = (bf16[576,144]{0,1:T(8,128)(2,1)}, bf16[576,144]{0,1:T(8,128)(2,1)S(1)}, u32[]{:S(2)}, u32[]{:S(2)}) collective-permute-start(bf16[576,144]{0,1:T(8,128)(2,1)} %get-tuple-element.54), channel_id=1, source_target_pairs={{0,7},{1,0},{2,1},{3,2},{4,3},{5,4},{6,5},{7,6},{8,15},{9,8},{10,9... | collective-permute-start | bytes 497672 | tf_op jit(solution)/shard_map/ppermute | solution.py:27
  413.4 8.6 %collective-permute-start.16 = (bf16[576,144]{0,1:T(8,128)(2,1)S(1)}, bf16[576,144]{0,1:T(8,128)(2,1)S(1)}, u32[]{:S(2)}, u32[]{:S(2)}) collective-permute-start(bf16[576,144]{0,1:T(8,128)(2,1)S(1)} %collective-permute-done.14), channel_id=1, source_target_pairs={{0,1},{1,2},{2,3},{3,4},{4,5},{5,6},{6,7},{7,0},{8,9},{9,10},{10,1... | collective-permute-start | bytes 497672 | tf_op jit(solution)/shard_map/ppermute | solution.py:22
  416.3 10.3 %collective-permute-start.17 = (bf16[576,144]{0,1:T(8,128)(2,1)S(1)}, bf16[576,144]{0,1:T(8,128)(2,1)S(1)}, u32[]{:S(2)}, u32[]{:S(2)}) collective-permute-start(bf16[576,144]{0,1:T(8,128)(2,1)S(1)} %collective-permute-done.15), channel_id=1, source_target_pairs={{0,7},{1,0},{2,1},{3,2},{4,3},{5,4},{6,5},{7,6},{8,15},{9,8},{10,9... | collective-permute-start | bytes 497672 | tf_op jit(solution)/shard_map/ppermute | solution.py:27
  539.0 160.4 %all-gather.14.cloned.1.call-start = ((), (), s32[]{:S(2)}) async-start(), calls=%async_computation.7 | async-start | bytes 5971968 | tf_op jit(solution)/shard_map/all_gather | solution.py:121
  539.8 211.8 %all-reduce.14.cloned.1.call-start = ((), (), s32[]{:S(2)}) async-start(), calls=%async_computation.5 | async-start | bytes 2064384 | tf_op jit(solution)/shard_map/psum | solution.py:177
  539.8 27.2 %collective-permute-start.21 = (bf16[2304,144]{0,1:T(8,128)(2,1)}, bf16[2304,144]{0,1:T(8,128)(2,1)S(1)}, u32[]{:S(2)}, u32[]{:S(2)}) collective-permute-start(bf16[2304,144]{0,1:T(8,128)(2,1)} %get-tuple-element.51), channel_id=1, source_target_pairs={{0,1},{1,2},{2,3},{3,4},{4,5},{5,6},{6,7},{7,0},{8,9},{9,10},{10,1... | collective-permute-start | bytes 1990664 | tf_op jit(solution)/shard_map/ppermute | solution.py:22
  540.2 29.3 %collective-permute-start.22 = (bf16[2304,144]{0,1:T(8,128)(2,1)}, bf16[2304,144]{0,1:T(8,128)(2,1)S(1)}, u32[]{:S(2)}, u32[]{:S(2)}) collective-permute-start(bf16[2304,144]{0,1:T(8,128)(2,1)} %get-tuple-element.51), channel_id=1, source_target_pairs={{0,7},{1,0},{2,1},{3,2},{4,3},{5,4},{6,5},{7,6},{8,15},{9,8},{10,9... | collective-permute-start | bytes 1990664 | tf_op jit(solution)/shard_map/ppermute | solution.py:27
  567.1 19.6 %collective-permute-start.23 = (bf16[2304,144]{0,1:T(8,128)(2,1)S(1)}, bf16[2304,144]{0,1:T(8,128)(2,1)S(1)}, u32[]{:S(2)}, u32[]{:S(2)}) collective-permute-start(bf16[2304,144]{0,1:T(8,128)(2,1)S(1)} %collective-permute-done.21), channel_id=1, source_target_pairs={{0,1},{1,2},{2,3},{3,4},{4,5},{5,6},{6,7},{7,0},{8,9},{9,10},{10,1... | collective-permute-start | bytes 1990664 | tf_op jit(solution)/shard_map/ppermute | solution.py:22
  569.5 35.6 %collective-permute-start.24 = (bf16[2304,144]{0,1:T(8,128)(2,1)S(1)}, bf16[2304,144]{0,1:T(8,128)(2,1)S(1)}, u32[]{:S(2)}, u32[]{:S(2)}) collective-permute-start(bf16[2304,144]{0,1:T(8,128)(2,1)S(1)} %collective-permute-done.22), channel_id=1, source_target_pairs={{0,7},{1,0},{2,1},{3,2},{4,3},{5,4},{6,5},{7,6},{8,15},{9,8},{10,9... | collective-permute-start | bytes 1990664 | tf_op jit(solution)/shard_map/ppermute | solution.py:27
  586.7 46.0 %collective-permute-start.25 = (bf16[2304,144]{0,1:T(8,128)(2,1)S(1)}, bf16[2304,144]{0,1:T(8,128)(2,1)S(1)}, u32[]{:S(2)}, u32[]{:S(2)}) collective-permute-start(bf16[2304,144]{0,1:T(8,128)(2,1)S(1)} %collective-permute-done.23), channel_id=1, source_target_pairs={{0,1},{1,2},{2,3},{3,4},{4,5},{5,6},{6,7},{7,0},{8,9},{9,10},{10,1... | collective-permute-start | bytes 1990664 | tf_op jit(solution)/shard_map/ppermute | solution.py:22
  605.1 47.8 %collective-permute-start.26 = (bf16[2304,144]{0,1:T(8,128)(2,1)S(1)}, bf16[2304,144]{0,1:T(8,128)(2,1)S(1)}, u32[]{:S(2)}, u32[]{:S(2)}) collective-permute-start(bf16[2304,144]{0,1:T(8,128)(2,1)S(1)} %collective-permute-done.24), channel_id=1, source_target_pairs={{0,7},{1,0},{2,1},{3,2},{4,3},{5,4},{6,5},{7,6},{8,15},{9,8},{10,9... | collective-permute-start | bytes 1990664 | tf_op jit(solution)/shard_map/ppermute | solution.py:27
  632.6 36.4 %collective-permute-start.27 = (bf16[2304,144]{0,1:T(8,128)(2,1)S(1)}, bf16[2304,144]{0,1:T(8,128)(2,1)S(1)}, u32[]{:S(2)}, u32[]{:S(2)}) collective-permute-start(bf16[2304,144]{0,1:T(8,128)(2,1)S(1)} %collective-permute-done.25), channel_id=1, source_target_pairs={{0,1},{1,2},{2,3},{3,4},{4,5},{5,6},{6,7},{7,0},{8,9},{9,10},{10,1... | collective-permute-start | bytes 1990664 | tf_op jit(solution)/shard_map/ppermute | solution.py:22
  (23 other events, 389.4 us)
Sparse Core Ops, SparseCore 0:
  42.0 77.3 all-reduce.15
  121.8 73.1 all-gather.7
  228.7 43.8 all-reduce.7
  274.9 113.6 all-gather.11
  399.7 41.2 all-reduce.9
  443.2 71.3 all-gather.9
  539.1 39.1 all-reduce.11
  580.7 118.6 all-gather.13
  711.2 40.3 all-reduce.13
